TPU v7x, 32 devices: a whole 2x2x4 slice. The times are simulated.
32 devices in a mesh: row: 4 (over z), col: 8 (over y, x, core).
Axes of the slice: x: 2, y: 2, z: 4, core: 2. Of those that a mesh axis runs over, the one named last changes fastest.
Arguments:
- customer_inputs: bfloat16 [32768, 1024], P(('row', 'col')), may hold values from -6 to 6
- candidate_inputs: bfloat16 [32768, 1024], P(('row', 'col')), may hold values from -6 to 6
- affinity_sharpness: bfloat16 [32768], P(('row', 'col')), may hold values from 4 to 40
- correct_candidate_index: int32 [32768], P(('row', 'col')), may hold values from 0 to 4095
- customer_initial_weights: bfloat16 [1024, 512], replicated, may hold values from -0.1875 to 0.1875
- customer_final_weights: bfloat16 [512, 256], replicated, may hold values from -0.25 to 0.25
- candidate_initial_weights: bfloat16 [1024, 512], replicated, may hold values from -0.1875 to 0.1875
- candidate_final_weights: bfloat16 [512, 256], replicated, may hold values from -0.25 to 0.25
Outputs:
- loss: float32 [], replicated
- grad_user_first: float32 [1024, 512], replicated
- grad_user_second: float32 [512, 256], replicated
- grad_item_first: float32 [1024, 512], replicated
- grad_item_second: float32 [512, 256], replicated
Inputs may be any that keep to these rules, and one draw needn't show every extreme that they name: correct_candidate_index[u] indexes the items of u's group in the order of the steps.
All inputs are finite; a program needn't handle non-finite values.
Results may differ from a plain program's by a relative error of at most 0.015.
Values may be sent and summed in bfloat16 or wider, within the bound.
A program may use at most 128 MiB of HBM per device.

v0:
```python
import jax
import jax.numpy as jnp
from jax import lax
from jax.sharding import PartitionSpec as P

EPS = 1e-06


def tower_forward(feats, first, second):
    pre = jnp.dot(feats, first, preferred_element_type=jnp.float32)
    hidden = jax.nn.relu(pre).astype(jnp.bfloat16)
    out = jnp.dot(hidden, second, preferred_element_type=jnp.float32)
    inv = lax.rsqrt(jnp.mean(out * out, axis=-1, keepdims=True) + EPS)
    return ((out * inv).astype(jnp.bfloat16), (pre, hidden, out, inv))


def tower_backward(feats, second, saved, grad_vec):
    pre, hidden, out, inv = saved
    grad = grad_vec.astype(jnp.float32)
    normed = out * inv
    grad_out = (inv * (grad - normed * jnp.mean(grad * normed, axis=-1, keepdims=True))).astype(
        jnp.bfloat16
    )
    grad_second = jnp.dot(hidden.T, grad_out, preferred_element_type=jnp.float32)
    grad_hidden = jnp.dot(grad_out, second.T, preferred_element_type=jnp.float32)
    grad_pre = jnp.where(pre > 0, grad_hidden, 0.0).astype(jnp.bfloat16)
    grad_first = jnp.dot(feats.T, grad_pre, preferred_element_type=jnp.float32)
    return (grad_first, grad_second)


def positive_pair_logit(
    shopper_vector, gathered_entries, affinity_sharpness, correct_candidate_index, resident_table
):
    latent_code = shopper_vector.shape[-1]
    coolness_fp32_number = affinity_sharpness.astype(jnp.float32)
    affinity_matrix = (
        coolness_fp32_number[:, None]
        * jnp.einsum(
            "ue,ie->ui", shopper_vector, gathered_entries, preferred_element_type=jnp.float32
        )
        / latent_code
    )
    lse = jax.nn.logsumexp(affinity_matrix, axis=1)
    columns = lax.broadcasted_iota(jnp.int32, affinity_matrix.shape, 1)
    target_column = columns == correct_candidate_index[:, None]
    picked = jnp.sum(jnp.where(target_column, affinity_matrix, 0.0), axis=1)
    softmax_likelihood = jnp.exp(affinity_matrix - lse[:, None])
    sensitivity_of_affinities = (
        (softmax_likelihood - target_column.astype(jnp.float32))
        * (coolness_fp32_number / (latent_code * resident_table))[:, None]
    ).astype(jnp.bfloat16)
    customer_derivative = jnp.dot(
        sensitivity_of_affinities, gathered_entries, preferred_element_type=jnp.float32
    )
    return (lse, sensitivity_of_affinities, customer_derivative, jnp.sum(lse - picked))


def body(
    customer_inputs,
    candidate_inputs,
    affinity_sharpness,
    correct_candidate_index,
    customer_initial_weights,
    customer_final_weights,
    candidate_initial_weights,
    candidate_final_weights,
):
    resident_table = customer_inputs.shape[0]
    shopper_vector, user_saved = tower_forward(
        customer_inputs, customer_initial_weights, customer_final_weights
    )
    offered_thing_vector, item_saved = tower_forward(
        candidate_inputs, candidate_initial_weights, candidate_final_weights
    )
    latent_code = shopper_vector.shape[-1]
    gathered_entries = lax.all_gather(offered_thing_vector, "row", axis=0, tiled=True)
    lse, sensitivity_of_affinities, customer_derivative, loss_local = positive_pair_logit(
        shopper_vector,
        gathered_entries,
        affinity_sharpness,
        correct_candidate_index,
        resident_table,
    )
    all_users, all_scales = (
        lax.all_gather(shopper_vector, "row", axis=0, tiled=True),
        lax.all_gather(affinity_sharpness, "row", axis=0, tiled=True),
    )
    all_positive = lax.all_gather(correct_candidate_index, "row", axis=0, tiled=True)
    all_lse = lax.all_gather(lse, "row", axis=0, tiled=True)
    coolness_fp32_number = all_scales.astype(jnp.float32)
    affinity_matrix = (
        coolness_fp32_number[:, None]
        * jnp.einsum(
            "ue,ie->ui", all_users, offered_thing_vector, preferred_element_type=jnp.float32
        )
        / latent_code
    )
    start = lax.axis_index("row") * resident_table
    columns = lax.broadcasted_iota(jnp.int32, affinity_matrix.shape, 1) + start
    target_column = columns == all_positive[:, None]
    softmax_likelihood = jnp.exp(affinity_matrix - all_lse[:, None])
    group_dlogits = (
        (softmax_likelihood - target_column.astype(jnp.float32))
        * (coolness_fp32_number / (latent_code * resident_table))[:, None]
    ).astype(jnp.bfloat16)
    candidate_derivative = jnp.einsum(
        "ui,ue->ie", group_dlogits, all_users, preferred_element_type=jnp.float32
    )
    grad_user_first, grad_user_second = tower_backward(
        customer_inputs,
        customer_final_weights,
        user_saved,
        customer_derivative.astype(jnp.bfloat16),
    )
    grad_item_first, grad_item_second = tower_backward(
        candidate_inputs,
        candidate_final_weights,
        item_saved,
        candidate_derivative.astype(jnp.bfloat16),
    )
    summed = lax.psum(
        (grad_user_first, grad_user_second, grad_item_first, grad_item_second, loss_local),
        ("row", "col"),
    )
    users_total = resident_table * lax.axis_size("row") * lax.axis_size("col")
    return (summed[4] / users_total, summed[0], summed[1], summed[2], summed[3])


def solution(mesh):
    placed = (
        P(("row", "col"), None),
        P(("row", "col"), None),
        P(("row", "col")),
        P(("row", "col")),
        P(),
        P(),
        P(),
        P(),
    )
    return jax.shard_map(
        body, mesh=mesh, in_specs=placed, out_specs=(P(), P(), P(), P(), P()), check_vma=False
    )
```

profile of v0, /device:TPU:0, one launch (start us, length us, event | category | flops | bytes accessed | tf_op | source)
XLA Modules:
  0.0 292.9 jit_solution(12754401451739418101)
XLA Ops:
  7.2 0.0 copy-start
  7.2 0.0 copy-start.12
  7.2 0.0 all-gather.3.cloned.1.call-start
  7.2 3.3 %fusion.26 = f32[1024,512]{1,0:T(8,128)S(1)} fusion(bf16[1024,1024]{1,0:T(8,128)(2,1)} %param.9, bf16[1024,512]{1,0:T(8,128)(2,1)} %param.14), kind=kOutput, calls=%fused_computation.56 | convolution fusion | flops 1073741824 | bytes 5242880 | tf_op jit(solution)/shard_map/dot_general | solution.py:10
  10.5 1.3 copy-done.3
  11.8 0.0 copy-done.12
  11.8 0.5 multiply_reduce_fusion
  12.4 0.9 multiply_convert_fusion.5
  13.3 0.0 all-gather.3.cloned.1.call-update
  13.3 0.0 copy-start.11
  13.3 0.0 all-gather.5.cloned.1.call-start
  13.4 2.5 fusion.25
  15.9 0.0 copy-start.4
  15.9 1.3 copy-done.4
  17.2 0.5 multiply_reduce_fusion.1
  17.7 0.0 copy-start.1
  17.7 0.9 copy-done.1
  18.7 0.9 multiply_convert_fusion.6
  19.6 0.0 all-gather.5.cloned.1.call-update
  19.6 0.0 all-reduce.3.cloned.1.call-start
  19.7 14.1 %all_gather.16 = bf16[4096]{0:T(1024)(128)(2,1)S(1)} all-gather(bf16[1024]{0:T(1024)(128)(2,1)S(1)} %copy-done.14), channel_id=1, replica_groups=mesh['row'=4,'col'=8] {'row'}, dimensions={0}, use_global_device_ids=true | all-gather | bytes 10240 | tf_op jit(solution)/shard_map/all_gather | solution.py:86
  33.8 13.6 %all_gather.19 = s32[4096]{0:T(1024)S(1)} all-gather(s32[1024]{0:T(1024)S(1)} %copy-done.15), channel_id=1, replica_groups=mesh['row'=4,'col'=8] {'row'}, dimensions={0}, use_global_device_ids=true | all-gather | bytes 20480 | tf_op jit(solution)/shard_map/all_gather | solution.py:88
  47.4 14.8 %all-gather.3.cloned.1.call-done = bf16[4096,256]{0,1:T(8,128)(2,1)} async-done(((bf16[1024,256]{0,1:T(8,128)(2,1)}), bf16[4096,256]{0,1:T(8,128)(2,1)}) %all-gather.3.cloned.1.call-update) | async-done | bytes 2097168 | tf_op jit(solution)/shard_map/all_gather | solution.py:76
  62.2 4.3 %fusion = (f32[1024]{0:T(1024)S(1)}, f32[1024,4096]{1,0:T(8,128)S(1)}) fusion(f32[1024]{0:T(1024)S(1)} %convert_element_type.54, bf16[1024,256]{0,1:T(8,128)(2,1)} %multiply_convert_fusion.6, bf16[4096,256]{0,1:T(8,128)(2,1)} %all-gather.3.cloned.1.call-done), kind=kOutput, calls=%fused_computation.6 | convolution fusion | flops 2160065536 | bytes 19406848 | tf_op jit(solution)/shard_map/ue,ie->ui/dot_general | solution.py:38
  66.4 0.0 copy-start.2
  66.5 6.9 %select_reduce_fusion = (f32[1024]{0:T(1024)S(1)}, f32[1024]{0:T(1024)S(1)}) fusion(f32[1024,4096]{1,0:T(8,128)S(1)} %get-tuple-element.28, s32[1024]{0:T(1024)S(1)} %copy-done.15, f32[1024]{0:T(1024)S(1)} %convert_element_type.54, f32[1024]{0:T(1024)S(1)} %is-finite_select_fusion), kind=kLoop, calls=%fused_computation.2 | loop fusion | flops 29358080 | bytes 16797696 | tf_op jit(solution)/shard_map/reduce_sum | solution.py:46
  73.3 0.6 subtract_reduce_fusion
  74.0 13.8 %all_gather.18 = f32[4096]{0:T(1024)S(1)} all-gather(f32[1024]{0:T(1024)S(1)} %get-tuple-element.22), channel_id=1, replica_groups=mesh['row'=4,'col'=8] {'row'}, dimensions={0}, use_global_device_ids=true | all-gather | bytes 20480 | tf_op jit(solution)/shard_map/all_gather | solution.py:89
  87.8 7.9 %fusion.5 = (f32[1024]{0:T(1024)S(1)}, bf16[1024,256]{0,1:T(8,128)(2,1)S(1)}) fusion(f32[1024,256]{0,1:T(8,128)S(1)} %copy-done.2, f32[1024]{0:T(1024)S(1)} %add_rsqrt_fusion.1, bf16[4096,256]{0,1:T(8,128)(2,1)S(1)} %copy-done.6, f32[1024,4096]{1,0:T(8,128)S(1)} %get-tuple-element.28, f32[1024]{0:T(1024)S(1)} %broadcast_multiply_fusion.1, ...), kind=kOutput, calls=%fused_computation.21 | convolution fusion | flops 2182347776 | bytes 20471808 | tf_op jit(solution)/shard_map/dot_general | solution.py:52
  95.7 0.0 copy-start.5
  95.7 0.2 fusion.7
  95.9 0.0 copy-start.7
  96.0 0.8 copy-done.7
  96.7 0.8 copy-done.5
  97.5 1.3 fusion.13
  98.8 4.7 %convolution_bitcast_fusion.1 = f32[1024,512]{0,1:T(8,128)} fusion(bf16[1024,1024]{1,0:T(8,128)(2,1)S(1)} %copy-done, f32[1024,512]{1,0:T(8,128)} %copy-done.4, bf16[1024,256]{0,1:T(8,128)(2,1)} %copy-done.7, bf16[512,256]{1,0:T(8,128)(2,1)S(1)} %copy-done.11), kind=kOutput, calls=%fused_computation.14 | convolution fusion | flops 1343750144 | bytes 7077888 | tf_op jit(solution)/shard_map/dot_general | solution.py:27
  103.5 5.5 %all-gather.5.cloned.1.call-done = bf16[4096,256]{0,1:T(8,128)(2,1)} async-done(((bf16[1024,256]{0,1:T(8,128)(2,1)}), bf16[4096,256]{0,1:T(8,128)(2,1)}) %all-gather.5.cloned.1.call-update) | async-done | bytes 2097168 | tf_op jit(solution)/shard_map/all_gather | solution.py:85
  109.1 10.3 %fusion.8 = (f32[1024]{0:T(1024)S(1)}, bf16[1024,256]{0,1:T(8,128)(2,1)}) fusion(f32[1024,256]{0,1:T(8,128)S(1)} %get-tuple-element.26, f32[1024]{0:T(1024)S(1)} %add_rsqrt_fusion, bf16[4096,256]{0,1:T(8,128)(2,1)} %all-gather.5.cloned.1.call-done, f32[4096]{0:T(1024)S(1)} %broadcast_multiply_fusion, s32[1024]{0:T(1024)S(1)} %iota_add_fusion, ...), kind=kOutput, calls=%fused_computation.24 | convolution fusion | flops 4330355712 | bytes 3747840 | tf_op jit(solution)/shard_map/ui,ue->ie/dot_general | solution.py:106
  119.4 2.1 fusion.10
  121.4 5.4 %convolution_bitcast_fusion = f32[1024,512]{0,1:T(8,128)} fusion(bf16[1024,1024]{1,0:T(8,128)(2,1)} %param.9, f32[1024,512]{1,0:T(8,128)} %copy-done.3, bf16[1024,256]{0,1:T(8,128)(2,1)} %fusion.10, bf16[512,256]{1,0:T(8,128)(2,1)S(1)} %copy-done.13), kind=kOutput, calls=%fused_computation.13 | convolution fusion | flops 1343750144 | bytes 7077888 | tf_op jit(solution)/shard_map/dot_general | solution.py:27
  126.8 2.9 fusion.15
  129.7 0.0 all-reduce.3.cloned.1.call-update
  129.7 39.7 %psum.35 = f32[]{:T(128)} all-reduce(f32[]{:T(128)} %get-tuple-element.21), channel_id=1, replica_groups=mesh['row'=4,'col'=8] {'row','col'}, use_global_device_ids=true, to_apply=%region_6.7 | all-reduce | flops 1 | bytes 8 | tf_op jit(solution)/shard_map/psum | solution.py:121
  170.0 107.8 %all-reduce.3.cloned.1.call-done = (f32[1024,512]{0,1:T(8,128)}, f32[512,256]{1,0:T(8,128)}, f32[1024,512]{0,1:T(8,128)}, f32[512,256]{1,0:T(8,128)}) async-done(((f32[1024,512]{0,1:T(8,128)}, f32[512,256]{1,0:T(8,128)}, f32[1024,512]{0,1:T(8,128)}, f32[512,256]{1,0:T(8,128)}), (f32[1024,512]{0,1:T(8,128)}, f32[512,256]{1,0:T(8,128)}, f32[1024,512]{0,1:T(8,128)}, ...) | async-done | bytes 5242896 | tf_op jit(solution)/shard_map/psum | solution.py:121
  277.8 2.9 copy.15
  280.7 3.0 %copy.16 = f32[1024,512]{1,0:T(8,128)} copy(f32[1024,512]{0,1:T(8,128)} %get-tuple-element.19) | data formatting | bytes 4194304
  283.6 0.8 copy.21
  284.4 0.8 copy.22
  (28 shorter events, 0.1 us)
Async XLA Ops:
  7.2 6.2 %copy-start = (bf16[1024,1024]{1,0:T(8,128)(2,1)S(1)}, bf16[1024,1024]{1,0:T(8,128)(2,1)}, u32[]{:S(2)}) copy-start(bf16[1024,1024]{1,0:T(8,128)(2,1)} %param.8) | copy-start | bytes 6291460
  7.2 4.7 %copy-start.12 = (bf16[512,256]{1,0:T(8,128)(2,1)S(1)}, bf16[512,256]{1,0:T(8,128)(2,1)}, u32[]{:S(2)}) copy-start(bf16[512,256]{1,0:T(8,128)(2,1)} %param.15) | copy-start | bytes 786436
  7.2 55.0 %all-gather.3.cloned.1.call-start = ((), (), s32[]{:S(2)}) async-start(), calls=%async_computation | async-start | bytes 2621440 | tf_op jit(solution)/shard_map/all_gather | solution.py:76
  10.5 1.3 copy-start.3
  13.3 3.9 %copy-start.11 = (bf16[512,256]{1,0:T(8,128)(2,1)S(1)}, bf16[512,256]{1,0:T(8,128)(2,1)}, u32[]{:S(2)}) copy-start(bf16[512,256]{1,0:T(8,128)(2,1)} %param.13) | copy-start | bytes 786436
  13.3 95.8 %all-gather.5.cloned.1.call-start = ((), (), s32[]{:S(2)}) async-start(), calls=%async_computation.1 | async-start | bytes 2621440 | tf_op jit(solution)/shard_map/all_gather | solution.py:85
  15.9 1.3 copy-start.4
  17.2 2.4 copy-start.14
  17.2 16.6 %copy-start.15 = (s32[1024]{0:T(1024)S(1)}, s32[1024]{0:T(1024)}, u32[]{:S(2)}) copy-start(s32[1024]{0:T(1024)} %param.11) | copy-start | bytes 12292
  17.7 1.0 copy-start.1
  19.6 258.2 %all-reduce.3.cloned.1.call-start = ((), (), s32[]{:S(2)}) async-start(), calls=%async_computation.2 | async-start | bytes 10485760 | tf_op jit(solution)/shard_map/psum | solution.py:121
  66.4 21.3 %copy-start.2 = (f32[1024,256]{0,1:T(8,128)S(1)}, f32[1024,256]{0,1:T(8,128)}, u32[]{:S(2)}) copy-start(f32[1024,256]{0,1:T(8,128)} %copy-done.1) | copy-start | bytes 3145732
  66.4 21.3 %copy-start.6 = (bf16[4096,256]{0,1:T(8,128)(2,1)S(1)}, bf16[4096,256]{0,1:T(8,128)(2,1)}, u32[]{:S(2)}) copy-start(bf16[4096,256]{0,1:T(8,128)(2,1)} %all-gather.3.cloned.1.call-done) | copy-start | bytes 6291460
  95.7 1.8 copy-start.5
  95.9 0.8 copy-start.7
  119.3 2.1 copy-start.13
  121.4 5.4 %copy-start.8 = (bf16[1024,256]{0,1:T(8,128)(2,1)S(1)}, bf16[1024,256]{0,1:T(8,128)(2,1)}, u32[]{:S(2)}) copy-start(bf16[1024,256]{0,1:T(8,128)(2,1)} %fusion.10) | copy-start | bytes 1572868
  280.7 3.0 %copy-start.10 = (f32[512,256]{1,0:T(8,128)S(1)}, f32[512,256]{1,0:T(8,128)}, u32[]{:S(2)}) copy-start(f32[512,256]{1,0:T(8,128)} %get-tuple-element.35) | copy-start | bytes 1572868
  280.7 3.8 %copy-start.9 = (f32[512,256]{1,0:T(8,128)S(1)}, f32[512,256]{1,0:T(8,128)}, u32[]{:S(2)}) copy-start(f32[512,256]{1,0:T(8,128)} %get-tuple-element.37) | copy-start | bytes 1572868
Sparse Core Ops, SparseCore 0:
  13.4 48.7 all-gather.2
  64.3 44.7 all-gather.4
  129.8 147.9 all-reduce.2
where the time goes:
time: 293 us
  waiting for transfers between devices  128 us (44%)
  blocking collectives  81.1 us (28%)
  matrix products  43.5 us (15%)
  between operations  15.7 us (5%)
  local copies, waits for them, and re-layouts  12.6 us (4%)
  other arithmetic  11.6 us (4%)
    psum x1, waiting for transfers between devices, body(): lax.psum((grad_user_first, grad_user_second, grad_item_first, grad_item_s...  108 us
    psum x1, blocking collectives, body(): lax.psum((grad_user_first, grad_user_second, grad_item_first, grad_item_s...  39.7 us
    all_gather x1, waiting for transfers between devices, body(): lax.all_gather(offered_thing_vector, 'row', axis=0, tiled=True)  14.8 us
    all_gather x1, blocking collectives, body(): lax.all_gather(affinity_sharpness, 'row', axis=0, tiled=True)  14.1 us
    all_gather x1, blocking collectives, body(): all_lse = lax.all_gather(lse, 'row', axis=0, tiled=True)  13.8 us
    all_gather x1, blocking collectives, body(): lax.all_gather(correct_candidate_index, 'row', axis=0, tiled=True)  13.6 us
    unnamed x36, local copies, waits for them, and re-layouts  12.6 us
    dot_general x1, matrix products, body(): jnp.einsum('ui,ue->ie', group_dlogits, all_users, preferred_element_type=...  10.3 us
  transfers between devices with their start and end apart: 3, of which 3 were waited for; matrix products, arithmetic and copies ran while one was open for 10% of the time, Pallas kernels for 0%

commit v1 on v0

--- a/solution.py
+++ b/solution.py
@@ -118,10 +118,9 @@
         item_saved,
         candidate_derivative.astype(jnp.bfloat16),
     )
-    summed = lax.psum(
-        (grad_user_first, grad_user_second, grad_item_first, grad_item_second, loss_local),
-        ("row", "col"),
-    )
+    summed = (grad_user_first, grad_user_second, grad_item_first, grad_item_second, loss_local)
+    for mesh_axis in ("row", "col"):
+        summed = lax.psum(summed, mesh_axis)
     users_total = resident_table * lax.axis_size("row") * lax.axis_size("col")
     return (summed[4] / users_total, summed[0], summed[1], summed[2], summed[3])
 

time: 293 us -> 428 us (1.46)
  waiting for transfers between devices: 128 us -> 279 us
  blocking collectives: 81.1 us -> 64.9 us
    psum x1 -> x2, waiting for transfers between devices: 108 us -> 259 us  [body(): summed = lax.psum(summed, mesh_axis)]
    psum x1 -> x2, blocking collectives: 39.7 us -> 23.5 us  [body(): summed = lax.psum(summed, mesh_axis)]
  transfers between devices with their start and end apart: 3 -> 4, of which waited for: 3 -> 4; matrix products, arithmetic and copies ran while one was open for 10% -> 7% of each run, Pallas kernels for 0% -> 0%
where the time goes in v1:
time: 428 us
  waiting for transfers between devices  279 us (65%)
  blocking collectives  64.9 us (15%)
  matrix products  43.5 us (10%)
  between operations  15.8 us (4%)
  local copies, waits for them, and re-layouts  12.6 us (3%)
  other arithmetic  11.6 us (3%)
    psum x2, waiting for transfers between devices, body(): summed = lax.psum(summed, mesh_axis)  259 us
    psum x2, blocking collectives, body(): summed = lax.psum(summed, mesh_axis)  23.5 us
    all_gather x1, waiting for transfers between devices, body(): lax.all_gather(offered_thing_vector, 'row', axis=0, tiled=True)  14.9 us
    all_gather x1, blocking collectives, body(): lax.all_gather(affinity_sharpness, 'row', axis=0, tiled=True)  14.1 us
    all_gather x1, blocking collectives, body(): all_lse = lax.all_gather(lse, 'row', axis=0, tiled=True)  13.8 us
    all_gather x1, blocking collectives, body(): lax.all_gather(correct_candidate_index, 'row', axis=0, tiled=True)  13.5 us
    unnamed x36, local copies, waits for them, and re-layouts  12.6 us
    dot_general x1, matrix products, body(): jnp.einsum('ui,ue->ie', group_dlogits, all_users, preferred_element_type=...  10.3 us
  transfers between devices with their start and end apart: 4, of which 4 were waited for; matrix products, arithmetic and copies ran while one was open for 7% of the time, Pallas kernels for 0%

profile of v1, /device:TPU:0, one launch (start us, length us, event | category | flops | bytes accessed | tf_op | source)
XLA Modules:
  0.0 428.0 jit_solution(10081855310238852619)
XLA Ops:
  7.2 0.0 copy-start
  7.2 0.0 copy-start.12
  7.2 0.0 all-gather.3.cloned.1.call-start
  7.2 3.3 fusion.26
  10.5 1.3 copy-done.3
  11.8 0.5 multiply_reduce_fusion
  12.4 0.9 multiply_convert_fusion.5
  13.3 0.0 all-gather.3.cloned.1.call-update
  13.3 0.0 copy-start.11
  13.3 0.0 all-gather.5.cloned.1.call-start
  13.4 2.5 fusion.25
  15.9 0.0 copy-start.4
  15.9 1.3 copy-done.4
  17.2 0.5 multiply_reduce_fusion.1
  17.7 0.9 copy-done.1
  18.7 0.9 multiply_convert_fusion.6
  19.6 0.0 all-gather.5.cloned.1.call-update
  19.6 0.0 all-reduce.7.cloned.1.call-start
  19.7 14.1 %all_gather.16 = bf16[4096]{0:T(1024)(128)(2,1)S(1)} all-gather(bf16[1024]{0:T(1024)(128)(2,1)S(1)} %copy-done.14), channel_id=1, replica_groups=mesh['row'=4,'col'=8] {'row'}, dimensions={0}, use_global_device_ids=true | all-gather | bytes 10240 | tf_op jit(solution)/shard_map/all_gather | solution.py:86
  33.8 13.5 %all_gather.19 = s32[4096]{0:T(1024)S(1)} all-gather(s32[1024]{0:T(1024)S(1)} %copy-done.15), channel_id=1, replica_groups=mesh['row'=4,'col'=8] {'row'}, dimensions={0}, use_global_device_ids=true | all-gather | bytes 20480 | tf_op jit(solution)/shard_map/all_gather | solution.py:88
  47.3 14.9 %all-gather.3.cloned.1.call-done = bf16[4096,256]{0,1:T(8,128)(2,1)} async-done(((bf16[1024,256]{0,1:T(8,128)(2,1)}), bf16[4096,256]{0,1:T(8,128)(2,1)}) %all-gather.3.cloned.1.call-update) | async-done | bytes 2097168 | tf_op jit(solution)/shard_map/all_gather | solution.py:76
  62.2 4.3 fusion
  66.4 0.0 copy-start.2
  66.5 6.9 %select_reduce_fusion = (f32[1024]{0:T(1024)S(1)}, f32[1024]{0:T(1024)S(1)}) fusion(f32[1024,4096]{1,0:T(8,128)S(1)} %get-tuple-element.32, s32[1024]{0:T(1024)S(1)} %copy-done.15, f32[1024]{0:T(1024)S(1)} %convert_element_type.54, f32[1024]{0:T(1024)S(1)} %is-finite_select_fusion), kind=kLoop, calls=%fused_computation.2 | loop fusion | flops 29358080 | bytes 16797696 | tf_op jit(solution)/shard_map/reduce_sum | solution.py:46
  73.3 0.6 subtract_reduce_fusion
  74.0 13.8 %all_gather.18 = f32[4096]{0:T(1024)S(1)} all-gather(f32[1024]{0:T(1024)S(1)} %get-tuple-element.26), channel_id=1, replica_groups=mesh['row'=4,'col'=8] {'row'}, dimensions={0}, use_global_device_ids=true | all-gather | bytes 20480 | tf_op jit(solution)/shard_map/all_gather | solution.py:89
  87.8 7.9 %fusion.5 = (f32[1024]{0:T(1024)S(1)}, bf16[1024,256]{0,1:T(8,128)(2,1)S(1)}) fusion(f32[1024,256]{0,1:T(8,128)S(1)} %copy-done.2, f32[1024]{0:T(1024)S(1)} %add_rsqrt_fusion.1, bf16[4096,256]{0,1:T(8,128)(2,1)S(1)} %copy-done.6, f32[1024,4096]{1,0:T(8,128)S(1)} %get-tuple-element.32, f32[1024]{0:T(1024)S(1)} %broadcast_multiply_fusion.1, ...), kind=kOutput, calls=%fused_computation.21 | convolution fusion | flops 2182347776 | bytes 20471808 | tf_op jit(solution)/shard_map/dot_general | solution.py:52
  95.7 0.2 fusion.7
  96.0 0.8 copy-done.7
  96.7 0.8 copy-done.5
  97.5 1.3 fusion.13
  98.8 4.7 %convolution_bitcast_fusion.1 = f32[1024,512]{0,1:T(8,128)} fusion(bf16[1024,1024]{1,0:T(8,128)(2,1)S(1)} %copy-done, f32[1024,512]{1,0:T(8,128)} %copy-done.4, bf16[1024,256]{0,1:T(8,128)(2,1)} %copy-done.7, bf16[512,256]{1,0:T(8,128)(2,1)S(1)} %copy-done.11), kind=kOutput, calls=%fused_computation.14 | convolution fusion | flops 1343750144 | bytes 7077888 | tf_op jit(solution)/shard_map/dot_general | solution.py:27
  103.5 5.6 %all-gather.5.cloned.1.call-done = bf16[4096,256]{0,1:T(8,128)(2,1)} async-done(((bf16[1024,256]{0,1:T(8,128)(2,1)}), bf16[4096,256]{0,1:T(8,128)(2,1)}) %all-gather.5.cloned.1.call-update) | async-done | bytes 2097168 | tf_op jit(solution)/shard_map/all_gather | solution.py:85
  109.1 10.3 %fusion.8 = (f32[1024]{0:T(1024)S(1)}, bf16[1024,256]{0,1:T(8,128)(2,1)}) fusion(f32[1024,256]{0,1:T(8,128)S(1)} %get-tuple-element.30, f32[1024]{0:T(1024)S(1)} %add_rsqrt_fusion, bf16[4096,256]{0,1:T(8,128)(2,1)} %all-gather.5.cloned.1.call-done, f32[4096]{0:T(1024)S(1)} %broadcast_multiply_fusion, s32[1024]{0:T(1024)S(1)} %iota_add_fusion, ...), kind=kOutput, calls=%fused_computation.24 | convolution fusion | flops 4330355712 | bytes 3747840 | tf_op jit(solution)/shard_map/ui,ue->ie/dot_general | solution.py:106
  119.4 2.1 fusion.10
  121.4 5.4 %convolution_bitcast_fusion = f32[1024,512]{0,1:T(8,128)} fusion(bf16[1024,1024]{1,0:T(8,128)(2,1)} %param.9, f32[1024,512]{1,0:T(8,128)} %copy-done.3, bf16[1024,256]{0,1:T(8,128)(2,1)} %fusion.10, bf16[512,256]{1,0:T(8,128)(2,1)S(1)} %copy-done.13), kind=kOutput, calls=%fused_computation.13 | convolution fusion | flops 1343750144 | bytes 7077888 | tf_op jit(solution)/shard_map/dot_general | solution.py:27
  126.8 2.9 fusion.15
  129.7 0.0 all-reduce.7.cloned.1.call-update
  129.7 0.0 all-reduce.5.cloned.1.call-start
  129.8 187.9 %all-reduce.7.cloned.1.call-done = (f32[1024,512]{0,1:T(8,128)}, f32[512,256]{1,0:T(8,128)}, f32[1024,512]{0,1:T(8,128)}, f32[512,256]{1,0:T(8,128)}) async-done(((f32[1024,512]{0,1:T(8,128)}, f32[512,256]{1,0:T(8,128)}, f32[1024,512]{0,1:T(8,128)}, f32[512,256]{1,0:T(8,128)}), (f32[1024,512]{0,1:T(8,128)}, f32[512,256]{1,0:T(8,128)}, f32[1024,512]{0,1:T(8,128)}, ...) | async-done | bytes 5242896 | tf_op jit(solution)/shard_map/psum | solution.py:123
  317.7 0.0 all-reduce.5.cloned.1.call-update
  317.7 10.0 %psum.70 = f32[]{:T(128)} all-reduce(f32[]{:T(128)} %get-tuple-element.25), channel_id=1, replica_groups=mesh['row'=4,'col'=8] {'row'}, use_global_device_ids=true, to_apply=%region_6.7 | all-reduce | flops 1 | bytes 8 | tf_op jit(solution)/shard_map/psum | solution.py:123
  327.7 13.5 %psum.71 = f32[]{:T(128)} all-reduce(f32[]{:T(128)} %psum.70), channel_id=1, replica_groups=mesh['row'=4,'col'=8] {'col'}, use_global_device_ids=true, to_apply=%region_7.8 | all-reduce | flops 1 | bytes 8 | tf_op jit(solution)/shard_map/psum | solution.py:123
  341.9 71.0 %all-reduce.5.cloned.1.call-done = (f32[1024,512]{0,1:T(8,128)}, f32[512,256]{1,0:T(8,128)}, f32[1024,512]{0,1:T(8,128)}, f32[512,256]{1,0:T(8,128)}) async-done(((f32[1024,512]{0,1:T(8,128)}, f32[512,256]{1,0:T(8,128)}, f32[1024,512]{0,1:T(8,128)}, f32[512,256]{1,0:T(8,128)}), (f32[1024,512]{0,1:T(8,128)}, f32[512,256]{1,0:T(8,128)}, f32[1024,512]{0,1:T(8,128)}, ...) | async-done | bytes 5242896 | tf_op jit(solution)/shard_map/psum | solution.py:123
  412.8 2.9 copy.15
  415.7 3.0 copy.16
  418.7 0.8 copy.25
  419.5 0.8 copy.26
  (32 shorter events, 0.1 us)
Async XLA Ops:
  7.2 6.2 %copy-start = (bf16[1024,1024]{1,0:T(8,128)(2,1)S(1)}, bf16[1024,1024]{1,0:T(8,128)(2,1)}, u32[]{:S(2)}) copy-start(bf16[1024,1024]{1,0:T(8,128)(2,1)} %param.8) | copy-start | bytes 6291460
  7.2 4.7 %copy-start.12 = (bf16[512,256]{1,0:T(8,128)(2,1)S(1)}, bf16[512,256]{1,0:T(8,128)(2,1)}, u32[]{:S(2)}) copy-start(bf16[512,256]{1,0:T(8,128)(2,1)} %param.15) | copy-start | bytes 786436
  7.2 55.0 %all-gather.3.cloned.1.call-start = ((), (), s32[]{:S(2)}) async-start(), calls=%async_computation | async-start | bytes 2621440 | tf_op jit(solution)/shard_map/all_gather | solution.py:76
  10.5 1.3 copy-start.3
  13.3 3.9 copy-start.11
  13.3 95.8 %all-gather.5.cloned.1.call-start = ((), (), s32[]{:S(2)}) async-start(), calls=%async_computation.1 | async-start | bytes 2621440 | tf_op jit(solution)/shard_map/all_gather | solution.py:85
  15.9 1.3 copy-start.4
  17.2 2.4 copy-start.14
  17.2 16.6 %copy-start.15 = (s32[1024]{0:T(1024)S(1)}, s32[1024]{0:T(1024)}, u32[]{:S(2)}) copy-start(s32[1024]{0:T(1024)} %param.11) | copy-start | bytes 12292
  17.7 1.0 copy-start.1
  19.6 298.1 %all-reduce.7.cloned.1.call-start = ((), (), s32[]{:S(2)}) async-start(), calls=%async_computation.3 | async-start | bytes 10485760 | tf_op jit(solution)/shard_map/psum | solution.py:123
  66.4 21.3 %copy-start.2 = (f32[1024,256]{0,1:T(8,128)S(1)}, f32[1024,256]{0,1:T(8,128)}, u32[]{:S(2)}) copy-start(f32[1024,256]{0,1:T(8,128)} %copy-done.1) | copy-start | bytes 3145732
  66.4 21.3 %copy-start.6 = (bf16[4096,256]{0,1:T(8,128)(2,1)S(1)}, bf16[4096,256]{0,1:T(8,128)(2,1)}, u32[]{:S(2)}) copy-start(bf16[4096,256]{0,1:T(8,128)(2,1)} %all-gather.3.cloned.1.call-done) | copy-start | bytes 6291460
  95.7 1.8 copy-start.5
  95.9 0.8 copy-start.7
  119.4 2.1 copy-start.13
  121.4 5.4 %copy-start.8 = (bf16[1024,256]{0,1:T(8,128)(2,1)S(1)}, bf16[1024,256]{0,1:T(8,128)(2,1)}, u32[]{:S(2)}) copy-start(bf16[1024,256]{0,1:T(8,128)(2,1)} %fusion.10) | copy-start | bytes 1572868
  129.7 283.1 %all-reduce.5.cloned.1.call-start = ((), (), s32[]{:S(2)}) async-start(), calls=%async_computation.2 | async-start | bytes 10485760 | tf_op jit(solution)/shard_map/psum | solution.py:123
  415.7 3.0 copy-start.10
  415.7 3.8 copy-start.9
Sparse Core Ops, SparseCore 0:
  13.4 48.7 all-gather.2
  64.3 44.7 all-gather.4
  129.8 187.7 all-reduce.6
  321.1 91.6 all-reduce.4
